TPU v7x, 256 devices: a whole 4x4x8 slice. The times are simulated.
256 devices in a mesh: chan: 32 (over z, x_hi, core), row: 4 (over y), col: 2 (over x_lo).
Axes of the slice: x: 4 (x_hi: 2, x_lo: 2; x = x_hi * 2 + x_lo), y: 4, z: 8, core: 2. Of those that a mesh axis runs over, the one named last changes fastest.
Arguments:
- voltages: bfloat16 [1024, 262144], P('chan', ('row', 'col')), may hold values from -6 to 6
Outputs:
- visibilities: float32 [256, 2, 1024, 1024], P('chan', None, 'row', 'col')
All inputs are finite; a program needn't handle non-finite values.
Results may differ from a plain program's by a relative error of at most 0.0053.
Values may be sent and summed in bfloat16 or wider, within the bound.
No kernel may reach another device: no remote copies, remote signals or barrier semaphores. Data moves between devices by JAX's collectives and lax.ppermute only.
A program may use at most 128 MiB of HBM per device.

v0:
```python
import jax
import jax.numpy as jnp
from jax import lax
from jax.sharding import PartitionSpec as P

FFT_LEN = 512
TAPS = 8
CHANNELS = 256


def shifted(value, axis, by):
    length = lax.axis_size(axis)
    pairs = [(i, i + by) for i in range(length) if 0 <= i + by < length]
    return lax.ppermute(value, axis, pairs)


def window_table(taps, length):
    count = taps * length
    position = jnp.arange(count).astype(jnp.float32)
    offset = (position - count / 2 + 0.5) / length
    taper = 0.5 - 0.5 * jnp.cos(2.0 * jnp.pi * (position + 0.5) / count)
    values = jnp.sinc(offset) * taper
    values = values / jnp.sqrt(jnp.sum(values * values))
    return values.reshape(taps, length)


def fourier_table(channels, length):
    channel_index = jnp.arange(channels, dtype=jnp.int32)[:, None]
    sample_index = jnp.arange(length, dtype=jnp.int32)[None, :]
    phase = (channel_index * sample_index % length).astype(jnp.float32) * (2.0 * jnp.pi / length)
    return jnp.stack([jnp.cos(phase), -jnp.sin(phase)], axis=1).astype(jnp.bfloat16)


def per_device(voltages):
    local_inputs = voltages.shape[0]
    slot_spectra = voltages.shape[1] // FFT_LEN
    window = window_table(TAPS, FFT_LEN)
    table = fourier_table(CHANNELS, FFT_LEN)
    tail = voltages[:, (slot_spectra - TAPS + 1) * FFT_LEN :]
    earlier = shifted(tail, ("row", "col"), 1)
    extended = jnp.concatenate([earlier, voltages], axis=1).reshape(
        local_inputs, slot_spectra + TAPS - 1, FFT_LEN
    )
    total = jnp.zeros((local_inputs, slot_spectra, FFT_LEN), jnp.float32)
    for tap_index in range(TAPS):
        total = total + window[tap_index][None, None, :] * extended[
            :, tap_index : tap_index + slot_spectra, :
        ].astype(jnp.float32)
    filtered = total.astype(jnp.bfloat16)
    spectra = jnp.einsum(
        "kpn,isn->kpsi", table, filtered, preferred_element_type=jnp.float32
    ).astype(jnp.bfloat16)
    turned = lax.all_to_all(spectra, "chan", split_axis=0, concat_axis=3, tiled=True)
    inputs_all = turned.shape[3]
    row_count = lax.axis_size("row")
    col_count = lax.axis_size("col")
    row_block = inputs_all // row_count
    col_block = inputs_all // col_count
    spectra_total = slot_spectra * row_count * col_count
    row_start = lax.axis_index("row") * row_block
    col_start = lax.axis_index("col") * col_block
    piece = lax.all_gather(turned, ("row", "col"), axis=2, tiled=True)
    left = lax.dynamic_slice_in_dim(piece, row_start, row_block, 3)
    right = lax.dynamic_slice_in_dim(piece, col_start, col_block, 3)
    flipped = jnp.stack([left[:, 1], -left[:, 0]], axis=1)
    real_part = jnp.einsum("cpsi,cpsj->cij", left, right, preferred_element_type=jnp.float32)
    imag_part = jnp.einsum("cpsi,cpsj->cij", flipped, right, preferred_element_type=jnp.float32)
    summed = jnp.stack([real_part, imag_part], axis=1)
    return summed / spectra_total


def solution(mesh):
    placed = (P("chan", ("row", "col")),)
    return jax.shard_map(
        per_device,
        mesh=mesh,
        in_specs=placed,
        out_specs=P("chan", None, "row", "col"),
        check_vma=False,
    )
```

profile of v0, /device:TPU:1, one launch (start us, length us, event | category | flops | bytes accessed | tf_op | source)
XLA Modules:
  0.0 496.5 jit_solution(200310706514286712)
XLA Ops:
  6.5 0.0 all-gather.2.cloned.1.call-start
  6.5 1.0 slice.66
  7.5 4.0 collective-permute-start
  11.5 0.7 multiply_reduce_fusion
  12.2 2.2 negate_convert_fusion
  15.0 0.1 broadcast_divide_fusion
  15.1 0.6 collective-permute-done
  15.7 1.7 pad_maximum_fusion
  17.4 2.6 reshape.97
  20.1 11.7 %convert_bitcast_fusion = bf16[256,2,64,32]{0,2,1,3:T(8,128)(2,1)S(1)} fusion(bf16[32,71,512]{2,1,0:T(8,128)(2,1)} %reshape.97, f32[512]{0:T(512)S(1)} %get-tuple-element.8, f32[512]{0:T(512)S(1)} %get-tuple-element.9, f32[512]{0:T(512)S(1)} %get-tuple-element.10, f32[512]{0:T(512)S(1)} %get-tuple-element.11, f32[512]{0:T(512)S(1)} %get-tuple-element.12, ...), kind=kOutput, calls=%fused_computation.16 | convolution fusion | flops 1101004800 | bytes 19415040 | tf_op jit(solution)/shard_map/kpn,isn->kpsi/dot_general | solution.py:50
  31.8 7.6 %copy.12 = bf16[256,2,64,32]{2,1,3,0:T(2,128)(2,1)} copy(bf16[256,2,64,32]{0,2,1,3:T(8,128)(2,1)S(1)} %convert_bitcast_fusion) | data formatting | bytes 4194304 | tf_op jit(solution)/shard_map/convert_element_type | solution.py:52
  39.5 9.1 %reshape.102 = bf16[32,2,16384]{2,1,0:T(2,128)(2,1)S(1)} reshape(bf16[256,32,2,64]{3,2,1,0:T(2,128)(2,1)} %bitcast.26) | data formatting | bytes 4194304
  48.6 62.7 %all_to_all.18 = bf16[32,2,16384]{2,1,0:T(2,128)(2,1)} all-to-all(bf16[32,2,16384]{2,1,0:T(2,128)(2,1)S(1)} %reshape.102), channel_id=1, replica_groups=mesh['chan'=32,'row'=4,'col'=2] {'chan'}, dimensions={0} | all-to-all | bytes 4194304 | tf_op jit(solution)/shard_map/all_to_all | solution.py:53
  111.3 9.8 %reshape.103 = bf16[256,32,2,64]{3,2,1,0:T(2,128)(2,1)} reshape(bf16[32,2,16384]{2,1,0:T(2,128)(2,1)} %all_to_all.18) | data formatting | bytes 4194304
  121.1 3.2 copy.13
  124.3 2.9 copy.14
  127.2 4.8 copy.15
  132.0 0.0 all-gather.2.cloned.1.call-update
  132.0 327.7 %all-gather.2.cloned.1.call-done = bf16[8,2,512,1024]{3,2,1,0:T(8,128)(2,1)} async-done(((bf16[8,2,64,1024]{3,2,1,0:T(8,128)(2,1)}), bf16[8,2,512,1024]{3,2,1,0:T(8,128)(2,1)}) %all-gather.2.cloned.1.call-update) | async-done | bytes 16777232 | tf_op jit(solution)/shard_map/all_gather | solution.py:62
  459.7 4.1 constant_dynamic-slice_fusion
  463.8 0.0 copy-start
  463.8 9.4 %fusion.8 = f32[8,1,256,512]{3,2,0,1:T(8,128)} fusion(bf16[8,2,512,1024]{3,2,1,0:T(8,128)(2,1)} %all-gather.2.cloned.1.call-done, s32[]{:T(128)S(6)} %select_n.65, s32[]{:T(128)S(6)} %select_n.64), kind=kOutput, calls=%fused_computation.11 | convolution fusion | flops 2147483648 | bytes 16777224 | tf_op jit(solution)/shard_map/cpsi,cpsj->cij/dot_general | solution.py:66
  473.2 1.6 copy-done
  474.7 6.0 %fusion.13 = f32[8,1,256,512]{3,2,0,1:T(8,128)} fusion(bf16[8,2,512,1024]{3,2,1,0:T(8,128)(2,1)S(1)} %copy-done, s32[]{:T(128)S(6)} %select_n.65, bf16[8,1,512,256]{3,2,1,0:T(8,128)(2,1)} %get-tuple-element.6, bf16[8,1,512,256]{3,2,1,0:T(8,128)(2,1)S(1)} %get-tuple-element.5), kind=kOutput, calls=%fused_computation.12 | convolution fusion | flops 2149580800 | bytes 16777220 | tf_op jit(solution)/shard_map/cpsi,cpsj->cij/dot_general | solution.py:67
  480.7 4.5 maximum_multiply_fusion
  485.2 4.4 copy.18
  (1 shorter events, 0.0 us)
Async XLA Ops:
  6.5 453.2 %all-gather.2.cloned.1.call-start = ((), (), s32[]{:S(2)}) async-start(), calls=%async_computation.1 | async-start | bytes 18874368 | tf_op jit(solution)/shard_map/all_gather | solution.py:62
  7.5 8.2 %collective-permute-start = (bf16[32,3584]{1,0:T(8,128)(2,1)S(1)}, bf16[32,3584]{1,0:T(8,128)(2,1)S(1)}, u32[]{:S(2)}, u32[]{:S(2)}) collective-permute-start(bf16[32,3584]{1,0:T(8,128)(2,1)S(1)} %slice.66), channel_id=1, source_target_pairs={{0,1},{1,2},{2,3},{3,4},{4,5},{5,6},{6,7},{8,9},{9,10},{10,11},{11... | collective-permute-start | bytes 688136 | tf_op jit(solution)/shard_map/ppermute | solution.py:14
  463.8 10.9 %copy-start = (bf16[8,2,512,1024]{3,2,1,0:T(8,128)(2,1)S(1)}, bf16[8,2,512,1024]{3,2,1,0:T(8,128)(2,1)}, u32[]{:S(2)}) copy-start(bf16[8,2,512,1024]{3,2,1,0:T(8,128)(2,1)} %all-gather.2.cloned.1.call-done) | copy-start | bytes 50331652
Sparse Core Ops, SparseCore 0:
  132.1 327.5 all-gather.1
where the time goes:
time: 497 us
  waiting for transfers between devices  328 us (66%)
  blocking collectives  62.7 us (13%)
  local copies, waits for them, and re-layouts  47.1 us (9%)
  matrix products  27.1 us (5%)
  between operations  14.2 us (3%)
  other arithmetic  13.3 us (3%)
    all_gather x1, waiting for transfers between devices, per_device(): piece = lax.all_gather(turned, ('row', 'col'), axis=2, tiled=True)  328 us
    all_to_all x1, blocking collectives, per_device(): lax.all_to_all(spectra, 'chan', split_axis=0, concat_axis=3, tiled=True)  62.7 us
    unnamed x4, local copies, waits for them, and re-layouts  20.5 us
    dot_general x1, matrix products, per_device(): jnp.einsum('kpn,isn->kpsi', table, filtered, preferred_element_type=jnp.f...  11.7 us
    all_to_all x3, local copies, waits for them, and re-layouts, per_device(): lax.all_to_all(spectra, 'chan', split_axis=0, concat_axis=3, tiled=True)  10.9 us
  transfers between devices with their start and end apart: 2, of which 2 were waited for; matrix products, arithmetic and copies ran while one was open for 1% of the time, Pallas kernels for 0%

commit v1 on v0

--- a/solution.py
+++ b/solution.py
@@ -59,7 +59,12 @@
     spectra_total = slot_spectra * row_count * col_count
     row_start = lax.axis_index("row") * row_block
     col_start = lax.axis_index("col") * col_block
-    piece = lax.all_gather(turned, ("row", "col"), axis=2, tiled=True)
+    all_rows = []
+    for _ in range(lax.axis_size(("row", "col"))):
+        all_rows.append(turned)
+    outcome_arr = jnp.stack(all_rows, 0)
+    v_now = lax.all_to_all(outcome_arr, ("row", "col"), 0, 0)
+    piece = jnp.concatenate(v_now, 2)
     left = lax.dynamic_slice_in_dim(piece, row_start, row_block, 3)
     right = lax.dynamic_slice_in_dim(piece, col_start, col_block, 3)
     flipped = jnp.stack([left[:, 1], -left[:, 0]], axis=1)

time: 497 us -> 352 us (0.71)
  waiting for transfers between devices: 328 us -> 184 us
  between operations: 14.2 us -> 0.78 us
  local copies, waits for them, and re-layouts: 47.1 us -> 58.4 us
  starting transfers between devices: 3.96 us -> 10.3 us
  matrix products: 27.1 us -> 21.9 us
    all_gather x1 -> x0, waiting for transfers between devices: 328 us -> none  [per_device(): piece = lax.all_gather(turned, ('row', 'col'), axis=2, tiled=True)]
    all_to_all x0 -> x1, waiting for transfers between devices: none -> 184 us  [per_device(): v_now = lax.all_to_all(outcome_arr, ('row', 'col'), 0, 0)]
    another operation x0 -> x2, local copies, waits for them, and re-layouts: none -> 9.52 us  [per_device(): outcome_arr = jnp.stack(all_rows, 0)]
    reshape x0 -> x1, local copies, waits for them, and re-layouts: none -> 8.15 us  [per_device(): piece = jnp.concatenate(v_now, 2)]
    all_to_all x0 -> x1, starting transfers between devices: none -> 6.37 us  [per_device(): v_now = lax.all_to_all(outcome_arr, ('row', 'col'), 0, 0)]
    dot_general x1, matrix products: 9.38 us -> 4.33 us  [per_device(): jnp.einsum('cpsi,cpsj->cij', left, right, preferred_element_type=jnp.floa...]
    all_to_all x3 -> x2, local copies, waits for them, and re-layouts: 10.9 us -> 6.16 us  [per_device(): lax.all_to_all(spectra, 'chan', split_axis=0, concat_axis=3, tiled=True)]
    unnamed x4 -> x2, local copies, waits for them, and re-layouts: 20.5 us -> 18.9 us
where the time goes in v1:
time: 352 us; the launch traced here: 350 us
  waiting for transfers between devices  184 us (52%)
  blocking collectives  62.8 us (18%)
  local copies, waits for them, and re-layouts  58.4 us (17%)
  matrix products  21.9 us (6%)
  other arithmetic  11.4 us (3%)
  starting transfers between devices  10.3 us (3%)
    all_to_all x1, waiting for transfers between devices, per_device(): v_now = lax.all_to_all(outcome_arr, ('row', 'col'), 0, 0)  184 us
    all_to_all x1, blocking collectives, per_device(): lax.all_to_all(spectra, 'chan', split_axis=0, concat_axis=3, tiled=True)  62.8 us
    unnamed x2, local copies, waits for them, and re-layouts  18.9 us
    dot_general x1, matrix products, per_device(): jnp.einsum('kpn,isn->kpsi', table, filtered, preferred_element_type=jnp.f...  11.6 us
    another operation x2, local copies, waits for them, and re-layouts, per_device(): outcome_arr = jnp.stack(all_rows, 0)  9.52 us
    reshape x1, local copies, waits for them, and re-layouts, per_device(): piece = jnp.concatenate(v_now, 2)  8.15 us
    convert_element_type x1, local copies, waits for them, and re-layouts, per_device(): spectra = jnp.einsum('kpn,isn->kpsi', table, filtered, preferred_element_...  7.64 us
  transfers between devices with their start and end apart: 2, of which 2 were waited for; matrix products, arithmetic and copies ran while one was open for 1% of the time, Pallas kernels for 0%

profile of v1, /device:TPU:1, one launch (start us, length us, event | category | flops | bytes accessed | tf_op | source)
XLA Modules:
  0.0 350.1 jit_solution(14333400283281498731)
XLA Ops:
  0.0 1.0 slice.66
  1.0 4.0 %collective-permute-start = (bf16[32,3584]{1,0:T(8,128)(2,1)S(1)}, bf16[32,3584]{1,0:T(8,128)(2,1)S(1)}, u32[]{:S(2)}, u32[]{:S(2)}) collective-permute-start(bf16[32,3584]{1,0:T(8,128)(2,1)S(1)} %slice.66), channel_id=1, source_target_pairs={{0,1},{1,2},{2,3},{3,4},{4,5},{5,6},{6,7},{8,9},{9,10},{10,11},{11... | collective-permute-start | bytes 688136 | tf_op jit(solution)/shard_map/ppermute | solution.py:14
  4.9 0.7 multiply_reduce_fusion
  5.6 2.2 negate_convert_fusion
  8.5 0.1 broadcast_divide_fusion
  8.6 0.6 collective-permute-done
  9.2 1.7 pad_maximum_fusion
  10.9 2.6 reshape.106
  13.6 11.6 %convert_bitcast_fusion = bf16[256,2,64,32]{0,2,1,3:T(8,128)(2,1)S(1)} fusion(bf16[32,71,512]{2,1,0:T(8,128)(2,1)} %reshape.106, f32[512]{0:T(512)S(1)} %get-tuple-element.8, f32[512]{0:T(512)S(1)} %get-tuple-element.9, f32[512]{0:T(512)S(1)} %get-tuple-element.10, f32[512]{0:T(512)S(1)} %get-tuple-element.11, f32[512]{0:T(512)S(1)} %get-tuple-element.12, ...), kind=kOutput, calls=%fused_computation.16 | convolution fusion | flops 1101004800 | bytes 19415040 | tf_op jit(solution)/shard_map/kpn,isn->kpsi/dot_general | solution.py:50
  25.2 7.6 %copy.11 = bf16[256,2,64,32]{2,1,3,0:T(2,128)(2,1)} copy(bf16[256,2,64,32]{0,2,1,3:T(8,128)(2,1)S(1)} %convert_bitcast_fusion) | data formatting | bytes 4194304 | tf_op jit(solution)/shard_map/convert_element_type | solution.py:52
  32.8 9.1 %reshape.113 = bf16[32,2,16384]{2,1,0:T(2,128)(2,1)S(1)} reshape(bf16[256,32,2,64]{3,2,1,0:T(2,128)(2,1)} %bitcast.31) | data formatting | bytes 4194304
  41.9 62.8 %all_to_all.20 = bf16[32,2,16384]{2,1,0:T(2,128)(2,1)} all-to-all(bf16[32,2,16384]{2,1,0:T(2,128)(2,1)S(1)} %reshape.113), channel_id=1, replica_groups=mesh['chan'=32,'row'=4,'col'=2] {'chan'}, dimensions={0} | all-to-all | bytes 4194304 | tf_op jit(solution)/shard_map/all_to_all | solution.py:53
  104.8 9.8 %reshape.114 = bf16[256,32,2,64]{3,2,1,0:T(2,128)(2,1)} reshape(bf16[32,2,16384]{2,1,0:T(2,128)(2,1)} %all_to_all.20) | data formatting | bytes 4194304
  114.5 3.2 copy.12
  117.8 2.9 copy.13
  120.7 3.5 %copy.14 = bf16[8,2,64,1024]{3,2,1,0:T(8,128)(2,1)S(1)} copy(bf16[8,2,64,1024]{2,3,1,0:T(8,128)(2,1)} %bitcast.34) | data formatting | bytes 4194304 | tf_op jit(solution)/shard_map/stack | solution.py:65
  124.3 6.0 %stack.34 = bf16[8,8,2,64,1024]{4,3,2,1,0:T(8,128)(2,1)} broadcast(bf16[8,2,64,1024]{3,2,1,0:T(8,128)(2,1)S(1)} %copy.14), dimensions={1,2,3,4} | broadcast | bytes 18874368 | tf_op jit(solution)/shard_map/stack | solution.py:65
  130.2 6.4 %all-to-all-start.1 = ((bf16[8,8,2,64,1024]{4,3,2,1,0:T(8,128)(2,1)}), bf16[8,8,2,64,1024]{4,3,2,1,0:T(8,128)(2,1)}, u32[]{:S(2)}, u32[]{:S(2)}) async-start(bf16[8,8,2,64,1024]{4,3,2,1,0:T(8,128)(2,1)} %stack.34), calls=%async_computation.1 | async-start | bytes 33554432 | tf_op jit(solution)/shard_map/all_to_all | solution.py:66
  136.6 183.8 %all-to-all-done.1 = bf16[8,8,2,64,1024]{4,3,2,1,0:T(8,128)(2,1)} async-done(((bf16[8,8,2,64,1024]{4,3,2,1,0:T(8,128)(2,1)}), bf16[8,8,2,64,1024]{4,3,2,1,0:T(8,128)(2,1)}, u32[]{:S(2)}, u32[]{:S(2)}) %all-to-all-start.1) | async-done | bytes 16777248 | tf_op jit(solution)/shard_map/all_to_all | solution.py:66
  320.4 8.1 %copy.15 = bf16[8,2,8,64,1024]{4,3,2,1,0:T(8,128)(2,1)S(1)} copy(bf16[8,2,8,64,1024]{4,3,1,0,2:T(8,128)(2,1)} %bitcast.7) | data formatting | bytes 33554432 | tf_op jit(solution)/shard_map/reshape | solution.py:67
  328.6 2.2 constant_dynamic-slice_fusion
  330.8 4.3 %fusion.8 = f32[8,1,256,512]{3,2,0,1:T(8,128)} fusion(bf16[8,2,512,1024]{3,2,1,0:T(8,128)(2,1)S(1)} %bitcast.29, s32[]{:T(128)S(6)} %select_n.65, s32[]{:T(128)S(6)} %select_n.64), kind=kOutput, calls=%fused_computation.11 | convolution fusion | flops 2147483648 | bytes 16777224 | tf_op jit(solution)/shard_map/cpsi,cpsj->cij/dot_general | solution.py:71
  335.1 6.0 %fusion.13 = f32[8,1,256,512]{3,2,0,1:T(8,128)} fusion(bf16[8,2,512,1024]{3,2,1,0:T(8,128)(2,1)S(1)} %bitcast.30, s32[]{:T(128)S(6)} %select_n.65, bf16[8,1,512,256]{3,2,1,0:T(8,128)(2,1)} %get-tuple-element.6, bf16[8,1,512,256]{3,2,1,0:T(8,128)(2,1)S(1)} %get-tuple-element.5), kind=kOutput, calls=%fused_computation.12 | convolution fusion | flops 2149580800 | bytes 16777220 | tf_op jit(solution)/shard_map/cpsi,cpsj->cij/dot_general | solution.py:72
  341.1 4.5 %maximum_multiply_fusion = f32[8,2,256,512]{3,2,0,1:T(8,128)S(1)} fusion(f32[8,1,256,512]{3,2,0,1:T(8,128)} %fusion.13, f32[8,1,256,512]{3,2,0,1:T(8,128)} %fusion.8), kind=kLoop, calls=%fused_computation | loop fusion | flops 4194304 | bytes 16777216 | tf_op jit(solution)/shard_map/div | solution.py:74
  345.7 4.4 %copy.18 = f32[8,2,256,512]{3,2,1,0:T(8,128)} copy(f32[8,2,256,512]{3,2,0,1:T(8,128)S(1)} %maximum_multiply_fusion) | data formatting | bytes 16777216 | tf_op jit(solution)/shard_map/div | solution.py:74
  (1 shorter events, 0.0 us)
Async XLA Ops:
  1.0 8.2 %collective-permute-start = (bf16[32,3584]{1,0:T(8,128)(2,1)S(1)}, bf16[32,3584]{1,0:T(8,128)(2,1)S(1)}, u32[]{:S(2)}, u32[]{:S(2)}) collective-permute-start(bf16[32,3584]{1,0:T(8,128)(2,1)S(1)} %slice.66), channel_id=1, source_target_pairs={{0,1},{1,2},{2,3},{3,4},{4,5},{5,6},{6,7},{8,9},{9,10},{10,11},{11... | collective-permute-start | bytes 688136 | tf_op jit(solution)/shard_map/ppermute | solution.py:14
  130.2 190.2 %all-to-all-start.1 = ((bf16[8,8,2,64,1024]{4,3,2,1,0:T(8,128)(2,1)}), bf16[8,8,2,64,1024]{4,3,2,1,0:T(8,128)(2,1)}, u32[]{:S(2)}, u32[]{:S(2)}) async-start(bf16[8,8,2,64,1024]{4,3,2,1,0:T(8,128)(2,1)} %stack.34), calls=%async_computation.1 | async-start | bytes 33554432 | tf_op jit(solution)/shard_map/all_to_all | solution.py:66
